TPU v7x, 512 devices: a whole 4x4x16 slice. The times are simulated.
512 devices in a mesh: dp: 128 (over z, x, core), mp: 4 (over y).
Axes of the slice: x: 4, y: 4, z: 16, core: 2. Of those that a mesh axis runs over, the one named last changes fastest.
Arguments:
- session_length: int32 [128], P('dp'), may hold values from 1 to 128
- event_owner: int32 [16384, 1], P('dp'), may hold values from 0 to 127; in each aligned block of 128 rows (0 to 127, 128 to 255, ...) at most 2 rows name the same one
- event_row: int32 [16384], P('dp'), may hold values from 0 to 255
- text_rows: bfloat16 [32768, 4096], P('dp', 'mp'), may hold values from -6 to 6
- image_rows: bfloat16 [32768, 4096], P('dp', 'mp'), may hold values from -6 to 6
- price: float32 [32768], P('dp'), may hold values from 0.2 to 5
- price_dir: bfloat16 [4096], P('mp'), may hold values from -4 to 4
- norm_gain: bfloat16 [4096], P('mp'), may hold values from 0.5 to 1.5
- w_query: bfloat16 [4096, 2048], P('dp', 'mp'), may hold values from -1 to 1
- w_key: bfloat16 [4096, 2048], P('dp', 'mp'), may hold values from -1 to 1
- w_value: bfloat16 [4096, 2048], P('dp', 'mp'), may hold values from -0.09375 to 0.09375
- cotangent: bfloat16 [16384, 4096], P('dp', 'mp'), may hold values from -6 to 6
Outputs:
- context: bfloat16 [16384, 2048], P('dp', 'mp')
- text_grad: float32 [32768, 4096], P('dp', 'mp')
- image_grad: float32 [32768, 4096], P('dp', 'mp')
Inputs may be any that keep to these rules, and one draw needn't show every extreme that they name: `event_owner`: among the event slots of one index of dp, no owner is named more than 2 times, a bound that some block reaches.
All inputs are finite; a program needn't handle non-finite values.
Results may differ from a plain program's by a relative error of at most 0.0063.
Values may be sent and summed in bfloat16 or wider, within the bound.
No kernel may reach another device: no remote copies, remote signals or barrier semaphores. Data moves between devices by JAX's collectives and lax.ppermute only.
A program may use at most 64 MiB of HBM per device.

v0:
```python
import math
import jax
import jax.numpy as jnp
from jax import lax
from jax.sharding import PartitionSpec as P

D = 4096
HD = 128
SLOT = 128


def fetch_rows(requests, text_rows, image_rows):
    row_ids = jnp.maximum(requests, 0)
    return (row_ids, text_rows[row_ids], image_rows[row_ids])


def join_rows(row_ids, text_got, image_got, price, price_dir):
    price_got = price[row_ids]
    mixed = text_got.astype(jnp.float32) * image_got.astype(jnp.float32) + price_got[
        ..., None
    ] * price_dir.astype(jnp.float32)
    return mixed.astype(jnp.bfloat16)


def answer(requests, text_rows, image_rows, price, price_dir):
    row_ids, text_got, image_got = fetch_rows(requests, text_rows, image_rows)
    joined_rows = join_rows(row_ids, text_got, image_got, price, price_dir)
    replies = lax.all_to_all(joined_rows, "dp", split_axis=0, concat_axis=0, tiled=True)
    return (replies, row_ids, text_got, image_got)


def credit_rows(row_ids, grad_rows, text_got, image_got, table_rows):
    col_width = grad_rows.shape[-1]
    flat_ids = row_ids.reshape(-1)
    grad_float = grad_rows.astype(jnp.float32)
    text_terms = (grad_float * image_got.astype(jnp.float32)).reshape(-1, col_width)
    image_terms = (grad_float * text_got.astype(jnp.float32)).reshape(-1, col_width)
    text_grad = jax.ops.segment_sum(text_terms, flat_ids, num_segments=table_rows)
    image_grad = jax.ops.segment_sum(image_terms, flat_ids, num_segments=table_rows)
    return (text_grad, image_grad)


def attend(query, keys, values, session_length):
    sessions = session_length.shape[0]
    heads_here = query.shape[1] // HD
    shape4 = (sessions, SLOT, heads_here, HD)
    scores = jnp.einsum(
        "sqhd,skhd->shqk",
        query.reshape(shape4),
        keys.reshape(shape4),
        preferred_element_type=jnp.float32,
    ) / math.sqrt(HD)
    position = jnp.arange(SLOT, dtype=jnp.int32)
    live_mask = position[None, :] < session_length[:, None]
    allowed = (position[None, :] <= position[:, None])[None, None, :, :] & live_mask[
        :, None, None, :
    ]
    scores = jnp.where(allowed, scores, jnp.float32(-1e30))
    row_max = jnp.max(scores, axis=-1, keepdims=True)
    powers = jnp.exp(scores - row_max)
    probs = (powers / jnp.sum(powers, axis=-1, keepdims=True)).astype(jnp.bfloat16)
    context = jnp.einsum(
        "shqk,skhd->sqhd", probs, values.reshape(shape4), preferred_element_type=jnp.float32
    )
    context = jnp.where(live_mask[:, :, None, None], context, jnp.float32(0.0))
    return context.reshape(sessions * SLOT, heads_here * HD).astype(jnp.bfloat16)


def local(
    session_length,
    event_owner,
    event_row,
    text_rows,
    image_rows,
    price,
    price_dir,
    norm_gain,
    w_query,
    w_key,
    w_value,
    cotangent,
):
    peers = lax.axis_size("dp")
    tok_count = event_row.shape[0]
    capacity = 2 * tok_count // peers
    col_width = text_rows.shape[1]
    table_rows = text_rows.shape[0]
    owner_ids = event_owner[:, 0]
    member = (owner_ids[:, None] == jnp.arange(peers, dtype=jnp.int32)[None, :]).astype(jnp.int32)
    earlier = jnp.sum((jnp.cumsum(member, axis=0) - member) * member, axis=1)
    slot_ids = owner_ids * capacity + earlier
    requests = (
        jnp.full((peers * capacity,), -1, jnp.int32)
        .at[slot_ids]
        .set(event_row)
        .reshape(peers, capacity)
    )
    grad_buffer = (
        jnp.zeros((peers * capacity, col_width), jnp.bfloat16)
        .at[slot_ids]
        .set(cotangent)
        .reshape(peers, capacity, col_width)
    )
    replies = answer(
        lax.all_to_all(requests, "dp", split_axis=0, concat_axis=0, tiled=True),
        text_rows,
        image_rows,
        price,
        price_dir,
    )[0]
    got_ids, got_grads = (
        lax.all_to_all(requests, "dp", split_axis=0, concat_axis=0, tiled=True),
        lax.all_to_all(grad_buffer, "dp", split_axis=0, concat_axis=0, tiled=True),
    )
    row_ids, text_got, image_got = fetch_rows(got_ids, text_rows, image_rows)
    text_grad, image_grad = credit_rows(row_ids, got_grads, text_got, image_got, table_rows)
    joined_rows = replies.reshape(peers * capacity, col_width)[slot_ids]
    joined_float = joined_rows.astype(jnp.float32)
    square_sums = lax.psum(jnp.sum(joined_float * joined_float, axis=1), "mp")
    scale = lax.rsqrt(square_sums / D + 1e-06)
    normed = (joined_float * scale[:, None] * norm_gain.astype(jnp.float32)[None, :]).astype(
        jnp.bfloat16
    )
    features_all = lax.all_gather(normed, "mp", axis=1, tiled=True)

    def add_rows(weight_rows):
        return jnp.dot(features_all, weight_rows, preferred_element_type=jnp.float32)

    query_sum = add_rows(lax.all_gather(w_query, "dp", axis=0, tiled=True))
    key_sum = add_rows(lax.all_gather(w_key, "dp", axis=0, tiled=True))
    value_sum = add_rows(lax.all_gather(w_value, "dp", axis=0, tiled=True))
    context = attend(
        query_sum.astype(jnp.bfloat16),
        key_sum.astype(jnp.bfloat16),
        value_sum.astype(jnp.bfloat16),
        session_length,
    )
    return (context, text_grad, image_grad)


def solution(mesh):
    return jax.shard_map(
        local,
        mesh=mesh,
        in_specs=(
            P("dp"),
            P("dp", None),
            P("dp"),
            P("dp", "mp"),
            P("dp", "mp"),
            P("dp"),
            P("mp"),
            P("mp"),
            P("dp", "mp"),
            P("dp", "mp"),
            P("dp", "mp"),
            P("dp", "mp"),
        ),
        out_specs=(P("dp", "mp"), P("dp", "mp"), P("dp", "mp")),
        check_vma=False,
    )
```

profile of v0, /device:TPU:1, one launch (start us, length us, event | category | flops | bytes accessed | tf_op | source)
XLA Modules:
  0.0 602.6 jit_solution(7912905382597587258)
XLA Ops:
  7.2 0.8 fusion.22
  8.2 0.8 select_reduce_fusion
  9.7 1.1 scatter_custom_fusion
  11.5 20.4 %all-to-all-start = ((s32[128,1,2]{2,1,0:T(1,128)}), s32[128,1,2]{2,1,0:T(1,128)S(1)}, u32[]{:S(2)}, u32[]{:S(2)}) async-start(s32[128,1,2]{2,1,0:T(1,128)} %bitcast.4), calls=%async_computation | async-start | bytes 131072 | tf_op jit(solution)/shard_map/all_to_all | solution.py:105
  31.9 1.7 scatter_custom_fusion.1
  33.7 1.0 reshape.139
  34.7 12.1 %all-to-all-done = s32[128,1,2]{2,1,0:T(1,128)S(1)} async-done(((s32[128,1,2]{2,1,0:T(1,128)}), s32[128,1,2]{2,1,0:T(1,128)S(1)}, u32[]{:S(2)}, u32[]{:S(2)}) %all-to-all-start) | async-done | bytes 1056 | tf_op jit(solution)/shard_map/all_to_all | solution.py:105
  46.8 5.7 all-to-all-start.2
  53.5 1.2 gather_fusion
  54.7 1.6 reshape.214
  56.3 1.9 gather_fusion.2
  58.4 1.2 gather_fusion.1
  59.6 1.6 reshape.215
  61.2 22.5 %all-to-all-done.2 = bf16[128,2,1024]{2,1,0:T(2,128)(2,1)S(1)} async-done(((bf16[128,2,1024]{2,1,0:T(2,128)(2,1)}), bf16[128,2,1024]{2,1,0:T(2,128)(2,1)S(1)}, u32[]{:S(2)}, u32[]{:S(2)}) %all-to-all-start.2) | async-done | bytes 524320 | tf_op jit(solution)/shard_map/all_to_all | solution.py:113
  83.7 3.1 convert_multiply_fusion
  86.9 9.2 %all-to-all-start.1 = ((bf16[128,2,1024]{2,1,0:T(2,128)(2,1)}), bf16[128,2,1024]{2,1,0:T(2,128)(2,1)}, u32[]{:S(2)}, u32[]{:S(2)}) async-start(bf16[128,2,1024]{2,1,0:T(2,128)(2,1)} %get-tuple-element.13), calls=%async_computation.1 | async-start | bytes 1048576 | tf_op jit(solution)/shard_map/all_to_all | solution.py:28
  96.4 30.2 %all-to-all-done.1 = bf16[128,2,1024]{2,1,0:T(2,128)(2,1)} async-done(((bf16[128,2,1024]{2,1,0:T(2,128)(2,1)}), bf16[128,2,1024]{2,1,0:T(2,128)(2,1)}, u32[]{:S(2)}, u32[]{:S(2)}) %all-to-all-start.1) | async-done | bytes 524320 | tf_op jit(solution)/shard_map/all_to_all | solution.py:28
  126.6 1.2 reshape.135
  127.8 0.9 gather_fusion.3
  128.8 8.7 %psum.7 = f32[128]{0:T(128)S(1)} all-reduce(f32[128]{0:T(128)S(1)} %fusion.8), channel_id=1, replica_groups=mesh['dp'=128,'mp'=4] {'mp'}, use_global_device_ids=true, to_apply=%region_4.5 | all-reduce | flops 128 | bytes 1024 | tf_op jit(solution)/shard_map/psum | solution.py:119
  137.6 0.8 fusion.10
  141.2 1.7 reshape.194
  143.6 4.3 scatter_custom_fusion.2
  147.9 3.6 scatter_custom_fusion.3
  151.5 11.5 %all-gather.5.cloned.1.call-done = bf16[128,4096]{1,0:T(8,128)(2,1)} async-done(((bf16[128,1024]{1,0:T(8,128)(2,1)}), bf16[128,4096]{1,0:T(8,128)(2,1)}) %all-gather.5.cloned.1.call-update) | async-done | bytes 1048592 | tf_op jit(solution)/shard_map/all_gather | solution.py:124
  163.0 146.8 %all-gather.7.cloned.1.call-done = bf16[4096,512]{1,0:T(8,128)(2,1)} async-done(((bf16[32,512]{1,0:T(8,128)(2,1)}), bf16[4096,512]{1,0:T(8,128)(2,1)}) %all-gather.7.cloned.1.call-update) | async-done | bytes 4194320 | tf_op jit(solution)/shard_map/all_gather | solution.py:131
  309.8 3.2 convolution_convert_fusion.2
  313.2 137.7 %all-gather.11.cloned.1.call-done = bf16[4096,512]{1,0:T(8,128)(2,1)} async-done(((bf16[32,512]{1,0:T(8,128)(2,1)}), bf16[4096,512]{1,0:T(8,128)(2,1)}) %all-gather.11.cloned.1.call-update) | async-done | bytes 4194320 | tf_op jit(solution)/shard_map/all_gather | solution.py:130
  450.9 2.9 fusion.7
  453.8 138.0 %all-gather.9.cloned.1.call-done = bf16[4096,512]{1,0:T(8,128)(2,1)} async-done(((bf16[32,512]{1,0:T(8,128)(2,1)}), bf16[4096,512]{1,0:T(8,128)(2,1)}) %all-gather.9.cloned.1.call-update) | async-done | bytes 4194320 | tf_op jit(solution)/shard_map/all_gather | solution.py:129
  591.9 2.9 fusion.6
  595.3 0.8 copy.30
  (37 shorter events, 6.6 us)
Async XLA Ops:
  7.2 46.3 %copy-start = (bf16[256,1024]{1,0:T(8,128)(2,1)S(1)}, bf16[256,1024]{1,0:T(8,128)(2,1)}, u32[]{:S(2)}) copy-start(bf16[256,1024]{1,0:T(8,128)(2,1)} %param.15) | copy-start | bytes 1572868
  11.5 35.2 %all-to-all-start = ((s32[128,1,2]{2,1,0:T(1,128)}), s32[128,1,2]{2,1,0:T(1,128)S(1)}, u32[]{:S(2)}, u32[]{:S(2)}) async-start(s32[128,1,2]{2,1,0:T(1,128)} %bitcast.4), calls=%async_computation | async-start | bytes 131072 | tf_op jit(solution)/shard_map/all_to_all | solution.py:105
  33.7 22.6 %copy-start.1 = (f32[256]{0:T(256)S(1)}, f32[256]{0:T(256)}, u32[]{:S(2)}) copy-start(f32[256]{0:T(256)} %param.17) | copy-start | bytes 3076
  46.8 37.0 %all-to-all-start.2 = ((bf16[128,2,1024]{2,1,0:T(2,128)(2,1)}), bf16[128,2,1024]{2,1,0:T(2,128)(2,1)S(1)}, u32[]{:S(2)}, u32[]{:S(2)}) async-start(bf16[128,2,1024]{2,1,0:T(2,128)(2,1)} %reshape.139), calls=%async_computation.2 | async-start | bytes 1048576 | tf_op jit(solution)/shard_map/all_to_all | solution.py:113
  56.3 2.1 copy-start.2
  59.6 36.8 %copy-start.4 = (bf16[1024]{0:T(1024)(128)(2,1)S(1)}, bf16[1024]{0:T(1024)(128)(2,1)}, u32[]{:S(2)}) copy-start(bf16[1024]{0:T(1024)(128)(2,1)} %param.19) | copy-start | bytes 6148
  86.9 39.7 %all-to-all-start.1 = ((bf16[128,2,1024]{2,1,0:T(2,128)(2,1)}), bf16[128,2,1024]{2,1,0:T(2,128)(2,1)}, u32[]{:S(2)}, u32[]{:S(2)}) async-start(bf16[128,2,1024]{2,1,0:T(2,128)(2,1)} %get-tuple-element.13), calls=%async_computation.1 | async-start | bytes 1048576 | tf_op jit(solution)/shard_map/all_to_all | solution.py:28
  96.1 66.9 %all-gather.5.cloned.1.call-start = ((), (), s32[]{:S(2)}) async-start(), calls=%async_computation.3 | async-start | bytes 1310720 | tf_op jit(solution)/shard_map/all_gather | solution.py:124
  138.4 171.4 %all-gather.7.cloned.1.call-start = ((), (), s32[]{:S(2)}) async-start(), calls=%async_computation.4 | async-start | bytes 4227072 | tf_op jit(solution)/shard_map/all_gather | solution.py:131
  139.2 311.8 %all-gather.11.cloned.1.call-start = ((), (), s32[]{:S(2)}) async-start(), calls=%async_computation.6 | async-start | bytes 4227072 | tf_op jit(solution)/shard_map/all_gather | solution.py:130
  139.9 452.0 %all-gather.9.cloned.1.call-start = ((), (), s32[]{:S(2)}) async-start(), calls=%async_computation.5 | async-start | bytes 4227072 | tf_op jit(solution)/shard_map/all_gather | solution.py:129
  163.0 287.9 %copy-start.3 = (bf16[128,4096]{1,0:T(8,128)(2,1)S(1)}, bf16[128,4096]{1,0:T(8,128)(2,1)}, u32[]{:S(2)}) copy-start(bf16[128,4096]{1,0:T(8,128)(2,1)} %all-gather.5.cloned.1.call-done) | copy-start | bytes 3145732
Sparse Core Ops, SparseCore 0:
  138.5 24.4 all-gather.4
  166.2 143.6 all-gather.6
  313.0 137.8 all-gather.10
  453.9 137.9 all-gather.8
where the time goes:
time: 603 us
  waiting for transfers between devices  501 us (83%)
  starting transfers between devices  35.6 us (6%)
  local copies, waits for them, and re-layouts  17.8 us (3%)
  other arithmetic  15.6 us (3%)
  between operations  14.6 us (2%)
  matrix products  9.46 us (2%)
  blocking collectives  8.72 us (1%)
    all_gather x1, waiting for transfers between devices, local(): value_sum = add_rows(lax.all_gather(w_value, 'dp', axis=0, tiled=True))  147 us
    all_gather x1, waiting for transfers between devices, local(): query_sum = add_rows(lax.all_gather(w_query, 'dp', axis=0, tiled=True))  138 us
    all_gather x1, waiting for transfers between devices, local(): key_sum = add_rows(lax.all_gather(w_key, 'dp', axis=0, tiled=True))  138 us
    all_to_all x1, waiting for transfers between devices, answer(): lax.all_to_all(joined_rows, 'dp', split_axis=0, concat_axis=0, tiled=True)  30.2 us
    all_to_all x1, waiting for transfers between devices, local(): lax.all_to_all(grad_buffer, 'dp', split_axis=0, concat_axis=0, tiled=True)  22.5 us
    all_to_all x1, starting transfers between devices, local(): lax.all_to_all(requests, 'dp', split_axis=0, concat_axis=0, tiled=True)  20.4 us
    all_to_all x1, waiting for transfers between devices, local(): lax.all_to_all(requests, 'dp', split_axis=0, concat_axis=0, tiled=True)  12.1 us
  transfers between devices with their start and end apart: 7, of which 7 were waited for; matrix products, arithmetic and copies ran while one was open for 5% of the time, Pallas kernels for 0%

commit v1 on v0

--- a/solution.py
+++ b/solution.py
@@ -7,6 +7,11 @@
 D = 4096
 HD = 128
 SLOT = 128
+
+
+def exchange_gather(x, name, d):
+    stack = jnp.stack([x] * lax.axis_size(name))
+    return jnp.concatenate(lax.all_to_all(stack, name, 0, 0), axis=d)
 
 
 def fetch_rows(requests, text_rows, image_rows):
@@ -126,7 +131,7 @@
     def add_rows(weight_rows):
         return jnp.dot(features_all, weight_rows, preferred_element_type=jnp.float32)
 
-    query_sum = add_rows(lax.all_gather(w_query, "dp", axis=0, tiled=True))
+    query_sum = add_rows(exchange_gather(w_query, "dp", 0))
     key_sum = add_rows(lax.all_gather(w_key, "dp", axis=0, tiled=True))
     value_sum = add_rows(lax.all_gather(w_value, "dp", axis=0, tiled=True))
     context = attend(

time: 603 us -> 510 us (0.85)
  waiting for transfers between devices: 501 us -> 393 us
  starting transfers between devices: 35.6 us -> 47.2 us
    all_gather x1 -> x0, waiting for transfers between devices: 138 us -> none  [local(): query_sum = add_rows(lax.all_gather(w_query, 'dp', axis=0, tiled=True))]
    all_gather x1, waiting for transfers between devices: 147 us -> 187 us  [local(): value_sum = add_rows(lax.all_gather(w_value, 'dp', axis=0, tiled=True))]
    all_to_all x0 -> x1, starting transfers between devices: none -> 11.6 us  [exchange_gather(): return jnp.concatenate(lax.all_to_all(stack, name, 0, 0), axis=d)]
    all_gather x1, waiting for transfers between devices: 11.5 us -> 0.01 us  [local(): features_all = lax.all_gather(normed, 'mp', axis=1, tiled=True)]
  transfers between devices with their start and end apart: 7 -> 7, of which waited for: 7 -> 5; matrix products, arithmetic and copies ran while one was open for 5% -> 6% of each run, Pallas kernels for 0% -> 0%
where the time goes in v1:
time: 510 us; the launch traced here: 509 us
  waiting for transfers between devices  393 us (77%)
  starting transfers between devices  47.2 us (9%)
  local copies, waits for them, and re-layouts  20.3 us (4%)
  other arithmetic  15.6 us (3%)
  between operations  14.6 us (3%)
  matrix products  9.47 us (2%)
  blocking collectives  8.72 us (2%)
    all_gather x1, waiting for transfers between devices, local(): value_sum = add_rows(lax.all_gather(w_value, 'dp', axis=0, tiled=True))  187 us
    all_gather x1, waiting for transfers between devices, local(): key_sum = add_rows(lax.all_gather(w_key, 'dp', axis=0, tiled=True))  140 us
    all_to_all x1, waiting for transfers between devices, answer(): lax.all_to_all(joined_rows, 'dp', split_axis=0, concat_axis=0, tiled=True)  30.2 us
    all_to_all x1, waiting for transfers between devices, local(): lax.all_to_all(grad_buffer, 'dp', split_axis=0, concat_axis=0, tiled=True)  22.5 us
    all_to_all x1, starting transfers between devices, local(): lax.all_to_all(requests, 'dp', split_axis=0, concat_axis=0, tiled=True)  20.4 us
    all_to_all x1, waiting for transfers between devices, local(): lax.all_to_all(requests, 'dp', split_axis=0, concat_axis=0, tiled=True)  12.1 us
    all_to_all x1, starting transfers between devices, exchange_gather(): return jnp.concatenate(lax.all_to_all(stack, name, 0, 0), axis=d)  11.6 us
  transfers between devices with their start and end apart: 7, of which 5 were waited for; matrix products, arithmetic and copies ran while one was open for 6% of the time, Pallas kernels for 0%

profile of v1, /device:TPU:1, one launch (start us, length us, event | category | flops | bytes accessed | tf_op | source)
XLA Modules:
  0.0 509.1 jit_solution(3765466944165506280)
XLA Ops:
  7.2 0.8 fusion.22
  8.2 0.8 select_reduce_fusion
  9.7 1.1 scatter_custom_fusion
  11.5 20.4 %all-to-all-start = ((s32[128,1,2]{2,1,0:T(1,128)}), s32[128,1,2]{2,1,0:T(1,128)S(1)}, u32[]{:S(2)}, u32[]{:S(2)}) async-start(s32[128,1,2]{2,1,0:T(1,128)} %bitcast.4), calls=%async_computation | async-start | bytes 131072 | tf_op jit(solution)/shard_map/all_to_all | solution.py:110
  31.9 1.7 scatter_custom_fusion.1
  33.7 1.0 reshape.145
  34.7 12.1 %all-to-all-done = s32[128,1,2]{2,1,0:T(1,128)S(1)} async-done(((s32[128,1,2]{2,1,0:T(1,128)}), s32[128,1,2]{2,1,0:T(1,128)S(1)}, u32[]{:S(2)}, u32[]{:S(2)}) %all-to-all-start) | async-done | bytes 1056 | tf_op jit(solution)/shard_map/all_to_all | solution.py:110
  46.8 5.7 %all-to-all-start.3 = ((bf16[128,2,1024]{2,1,0:T(2,128)(2,1)}), bf16[128,2,1024]{2,1,0:T(2,128)(2,1)S(1)}, u32[]{:S(2)}, u32[]{:S(2)}) async-start(bf16[128,2,1024]{2,1,0:T(2,128)(2,1)} %reshape.145), calls=%async_computation.3 | async-start | bytes 1048576 | tf_op jit(solution)/shard_map/all_to_all | solution.py:118
  53.5 1.2 gather_fusion
  54.7 1.6 reshape.220
  56.3 1.2 gather_fusion.1
  57.5 1.6 reshape.221
  59.1 1.9 gather_fusion.2
  61.2 22.5 %all-to-all-done.3 = bf16[128,2,1024]{2,1,0:T(2,128)(2,1)S(1)} async-done(((bf16[128,2,1024]{2,1,0:T(2,128)(2,1)}), bf16[128,2,1024]{2,1,0:T(2,128)(2,1)S(1)}, u32[]{:S(2)}, u32[]{:S(2)}) %all-to-all-start.3) | async-done | bytes 524320 | tf_op jit(solution)/shard_map/all_to_all | solution.py:118
  83.7 3.1 convert_multiply_fusion
  86.9 9.2 %all-to-all-start.1 = ((bf16[128,2,1024]{2,1,0:T(2,128)(2,1)}), bf16[128,2,1024]{2,1,0:T(2,128)(2,1)}, u32[]{:S(2)}, u32[]{:S(2)}) async-start(bf16[128,2,1024]{2,1,0:T(2,128)(2,1)} %get-tuple-element.13), calls=%async_computation.1 | async-start | bytes 1048576 | tf_op jit(solution)/shard_map/all_to_all | solution.py:33
  96.4 30.2 %all-to-all-done.1 = bf16[128,2,1024]{2,1,0:T(2,128)(2,1)} async-done(((bf16[128,2,1024]{2,1,0:T(2,128)(2,1)}), bf16[128,2,1024]{2,1,0:T(2,128)(2,1)}, u32[]{:S(2)}, u32[]{:S(2)}) %all-to-all-start.1) | async-done | bytes 524320 | tf_op jit(solution)/shard_map/all_to_all | solution.py:33
  126.6 1.2 reshape.140
  127.8 0.9 gather_fusion.3
  128.8 8.7 %psum.7 = f32[128]{0:T(128)S(1)} all-reduce(f32[128]{0:T(128)S(1)} %fusion.8), channel_id=1, replica_groups=mesh['dp'=128,'mp'=4] {'mp'}, use_global_device_ids=true, to_apply=%region_4.5 | all-reduce | flops 128 | bytes 1024 | tf_op jit(solution)/shard_map/psum | solution.py:124
  137.6 0.9 fusion.10
  139.2 2.5 stack.2
  141.7 11.6 %all-to-all-start.2 = ((bf16[128,32,512]{2,1,0:T(8,128)(2,1)}), bf16[128,32,512]{2,1,0:T(8,128)(2,1)}, u32[]{:S(2)}, u32[]{:S(2)}) async-start(bf16[128,32,512]{2,1,0:T(8,128)(2,1)} %stack.2), calls=%async_computation.2 | async-start | bytes 8388608 | tf_op jit(solution)/shard_map/all_to_all | solution.py:14
  154.8 1.7 reshape.200
  157.2 4.3 scatter_custom_fusion.2
  161.5 3.6 scatter_custom_fusion.3
  165.1 187.3 %all-gather.6.cloned.1.call-done = bf16[4096,512]{1,0:T(8,128)(2,1)} async-done(((bf16[32,512]{1,0:T(8,128)(2,1)}), bf16[4096,512]{1,0:T(8,128)(2,1)}) %all-gather.6.cloned.1.call-update) | async-done | bytes 4194320 | tf_op jit(solution)/shard_map/all_gather | solution.py:136
  352.4 3.2 convolution_convert_fusion.2
  355.8 139.7 %all-gather.8.cloned.1.call-done = bf16[4096,512]{1,0:T(8,128)(2,1)} async-done(((bf16[32,512]{1,0:T(8,128)(2,1)}), bf16[4096,512]{1,0:T(8,128)(2,1)}) %all-gather.8.cloned.1.call-update) | async-done | bytes 4194320 | tf_op jit(solution)/shard_map/all_gather | solution.py:135
  495.4 2.9 fusion.7
  498.3 2.9 fusion.6
  501.8 0.8 copy.30
  (39 shorter events, 6.1 us)
Async XLA Ops:
  7.2 46.3 %copy-start = (bf16[256,1024]{1,0:T(8,128)(2,1)S(1)}, bf16[256,1024]{1,0:T(8,128)(2,1)}, u32[]{:S(2)}) copy-start(bf16[256,1024]{1,0:T(8,128)(2,1)} %param.15) | copy-start | bytes 1572868
  11.5 35.2 %all-to-all-start = ((s32[128,1,2]{2,1,0:T(1,128)}), s32[128,1,2]{2,1,0:T(1,128)S(1)}, u32[]{:S(2)}, u32[]{:S(2)}) async-start(s32[128,1,2]{2,1,0:T(1,128)} %bitcast.4), calls=%async_computation | async-start | bytes 131072 | tf_op jit(solution)/shard_map/all_to_all | solution.py:110
  33.7 22.6 %copy-start.2 = (bf16[256,1024]{1,0:T(8,128)(2,1)S(1)}, bf16[256,1024]{1,0:T(8,128)(2,1)}, u32[]{:S(2)}) copy-start(bf16[256,1024]{1,0:T(8,128)(2,1)} %param.16) | copy-start | bytes 1572868
  46.8 37.0 %all-to-all-start.3 = ((bf16[128,2,1024]{2,1,0:T(2,128)(2,1)}), bf16[128,2,1024]{2,1,0:T(2,128)(2,1)S(1)}, u32[]{:S(2)}, u32[]{:S(2)}) async-start(bf16[128,2,1024]{2,1,0:T(2,128)(2,1)} %reshape.145), calls=%async_computation.3 | async-start | bytes 1048576 | tf_op jit(solution)/shard_map/all_to_all | solution.py:118
  54.7 4.4 copy-start.1
  61.0 35.3 %copy-start.5 = (bf16[1024]{0:T(1024)(128)(2,1)S(1)}, bf16[1024]{0:T(1024)(128)(2,1)}, u32[]{:S(2)}) copy-start(bf16[1024]{0:T(1024)(128)(2,1)} %param.19) | copy-start | bytes 6148
  61.2 78.0 %copy-start.4 = (bf16[32,512]{1,0:T(8,128)(2,1)S(1)}, bf16[32,512]{1,0:T(8,128)(2,1)}, u32[]{:S(2)}) copy-start(bf16[32,512]{1,0:T(8,128)(2,1)} %param.20) | copy-start | bytes 98308
  86.9 39.7 %all-to-all-start.1 = ((bf16[128,2,1024]{2,1,0:T(2,128)(2,1)}), bf16[128,2,1024]{2,1,0:T(2,128)(2,1)}, u32[]{:S(2)}, u32[]{:S(2)}) async-start(bf16[128,2,1024]{2,1,0:T(2,128)(2,1)} %get-tuple-element.13), calls=%async_computation.1 | async-start | bytes 1048576 | tf_op jit(solution)/shard_map/all_to_all | solution.py:33
  96.1 69.0 %all-gather.4.cloned.1.call-start = ((), (), s32[]{:S(2)}) async-start(), calls=%async_computation.4 | async-start | bytes 1310720 | tf_op jit(solution)/shard_map/all_gather | solution.py:129
  138.4 214.0 %all-gather.6.cloned.1.call-start = ((), (), s32[]{:S(2)}) async-start(), calls=%async_computation.5 | async-start | bytes 4227072 | tf_op jit(solution)/shard_map/all_gather | solution.py:136
  141.7 356.6 %all-to-all-start.2 = ((bf16[128,32,512]{2,1,0:T(8,128)(2,1)}), bf16[128,32,512]{2,1,0:T(8,128)(2,1)}, u32[]{:S(2)}, u32[]{:S(2)}) async-start(bf16[128,32,512]{2,1,0:T(8,128)(2,1)} %stack.2), calls=%async_computation.2 | async-start | bytes 8388608 | tf_op jit(solution)/shard_map/all_to_all | solution.py:14
  153.3 342.1 %all-gather.8.cloned.1.call-start = ((), (), s32[]{:S(2)}) async-start(), calls=%async_computation.6 | async-start | bytes 4227072 | tf_op jit(solution)/shard_map/all_gather | solution.py:135
  165.1 330.3 %copy-start.3 = (bf16[128,4096]{1,0:T(8,128)(2,1)S(1)}, bf16[128,4096]{1,0:T(8,128)(2,1)}, u32[]{:S(2)}) copy-start(bf16[128,4096]{1,0:T(8,128)(2,1)} %all-gather.4.cloned.1.call-done) | copy-start | bytes 3145732
Sparse Core Ops, SparseCore 0:
  138.6 24.4 all-gather.3
  166.2 186.1 all-gather.5
  355.5 139.8 all-gather.7
